TPU v7x, 256 devices: a whole 4x4x8 slice. The times are simulated.
256 devices in a mesh: pair: 32 (over z_lo, y, x), sector: 8 (over z_hi, core).
Axes of the slice: x: 4, y: 4, z: 8 (z_hi: 4, z_lo: 2; z = z_hi * 2 + z_lo), core: 2. Of those that a mesh axis runs over, the one named last changes fastest.
Arguments:
- wavefunction: float32 [8, 512, 512], P('sector', 'pair'), may hold values from -6 to 6
- preconditioner: float32 [8, 512, 512], P('sector', 'pair'), may hold values from 0.5 to 4
- left_ops: float32 [96, 8, 512, 512], P('pair', 'sector'), may hold values from -0.25 to 0.25
- right_ops: float32 [96, 8, 512, 512], P('pair', 'sector'), may hold values from -0.01953125 to 0.01953125
- charges: int32 [96], P('pair'), may hold values from 0 to 2
- coupling: int32 [8, 3], P('sector'), may hold values 0 or 1
Outputs:
- new_state: float32 [8, 512, 512], P('sector', 'pair')
- new_image: float32 [8, 512, 512], P('sector', 'pair')
- energies: float32 [2], replicated
All inputs are finite; a program needn't handle non-finite values. No bound on the sum of `coupling` on one device may be relied on, other than what follows from the above.
Results may differ from a plain program's by a relative error of at most 0.0003.
Values sent between devices are 32-bit elements; how exact they have to be, the bound alone decides.
A program may use at most 64 MiB of HBM per device.

v0:
```python
import math
import jax
import jax.numpy as jnp
from jax import lax
from jax.sharding import Mesh
from jax.sharding import PartitionSpec as P

SECTOR = ("sector_0", "sector_1")
PAIR = ("pair_0", "pair_1", "pair_2")
PAIR_SECTOR = ("pair_0", "pair_1", "pair_2", "sector_0", "sector_1")
highest = lax.Precision.HIGHEST


def shifted(block, axis, distance):
    devices = range(lax.axis_size(axis))
    route = [((i - distance) % len(devices), i) for i in devices]
    return lax.ppermute(block, axis, route)


def side_by_side(arrays, axis, dim, along):
    widths = [a.shape[along] for a in arrays]
    both = jnp.concatenate(arrays, axis=along)
    out = lax.all_gather(both, axis, axis=dim, tiled=True)
    return tuple(jnp.split(out, [sum(widths[:k]) for k in range(1, len(widths))], axis=along))


def cut_along(value, dim, peers):
    lengths = value.shape
    blocks = value.reshape(*lengths[:dim], peers, lengths[dim] // peers, *lengths[dim + 1 :])
    return jnp.moveaxis(blocks, dim, 0)


def sum_at_owner(value, axis, dim):
    peers = lax.axis_size(axis)
    blocks = lax.all_to_all(cut_along(value, dim, peers), axis, 0, 0, tiled=True)
    return jnp.sum(blocks, axis=0)


def by_axis(value, axes):
    for axis in axes:
        value = lax.psum(value, axis)
    return value


def product(first, second):
    return jnp.dot(first, second, precision=highest, preferred_element_type=jnp.float32)


def sigma_apply(vector, left_ops, right_ops, charges, coupling):
    lower_rows = shifted(vector, SECTOR, 1)
    upper_rows = shifted(vector, SECTOR, -1)
    gathered = side_by_side((lower_rows, vector, upper_rows), PAIR, 1, 0)
    stacked = jnp.concatenate(gathered, axis=0)
    own_block = stacked[1]
    targets = jnp.zeros_like(stacked)
    for which_pair in range(left_ops.shape[0]):
        left_block = left_ops[which_pair, 0]
        right_block = right_ops[which_pair, 0]
        charge_slot = charges[which_pair]
        allowed = lax.dynamic_index_in_dim(coupling[0], charge_slot, 0, keepdims=False).astype(
            jnp.float32
        )
        source_block = lax.dynamic_index_in_dim(stacked, charge_slot, 0, keepdims=False)
        forward = product(product(left_block, own_block), right_block.T)
        backward = product(product(left_block.T, source_block), right_block)
        current = lax.dynamic_index_in_dim(targets, charge_slot, 0, keepdims=False)
        targets = lax.dynamic_update_index_in_dim(
            targets, current + allowed * forward, charge_slot, 0
        )
        targets = targets.at[1].add(allowed * backward)
    from_below = shifted(targets[2], SECTOR, 1)
    from_above = shifted(targets[0], SECTOR, -1)
    combined = targets[1] + from_below + from_above
    return sum_at_owner(combined[None], PAIR, 1)


def per_device(wavefunction, preconditioner, left_ops, right_ops, charges, coupling):
    first_image = sigma_apply(wavefunction, left_ops, right_ops, charges, coupling)
    norm_sq, correlation = (
        by_axis(jnp.sum(wavefunction * wavefunction), PAIR_SECTOR),
        by_axis(jnp.sum(wavefunction * first_image), PAIR_SECTOR),
    )
    theta = correlation / norm_sq
    inverse = lax.rsqrt(norm_sq)
    vector = wavefunction * inverse
    image = first_image * inverse
    residual = image - theta * vector
    correction = residual / preconditioner
    along, squared = (
        by_axis(jnp.sum(vector * correction), PAIR_SECTOR),
        by_axis(jnp.sum(correction * correction), PAIR_SECTOR),
    )
    orthogonal = correction - along * vector
    length_sq = squared - along * along
    basis = orthogonal * lax.rsqrt(length_sq + 1e-30)
    second_image = sigma_apply(basis, left_ops, right_ops, charges, coupling)
    corner, cross = (
        by_axis(jnp.sum(basis * second_image), PAIR_SECTOR),
        by_axis(jnp.sum(vector * second_image), PAIR_SECTOR),
    )
    half = (theta - corner) / 2.0
    lowest = (theta + corner) / 2.0 - jnp.sqrt(half * half + cross * cross)
    first_weight = corner - lowest
    second_weight = -cross
    size_norm = jnp.sqrt(first_weight * first_weight + second_weight * second_weight + 1e-30)
    entries = (
        lax.axis_size(SECTOR) * lax.axis_size(PAIR) * wavefunction.shape[1] * wavefunction.shape[2]
    )
    scale = jnp.float32(math.sqrt(entries))
    factor_one = scale * first_weight / size_norm
    factor_two = scale * second_weight / size_norm
    new_state = factor_one * vector + factor_two * basis
    new_image = factor_one * image + factor_two * second_image
    energies = jnp.stack([theta, lowest])
    return (new_state, new_image, energies)


def solution(mesh):
    split = Mesh(
        mesh.devices.reshape(2, 4, 4, 4, 2), ("pair_0", "pair_1", "pair_2", "sector_0", "sector_1")
    )
    placed = (
        P(SECTOR, PAIR, None),
        P(SECTOR, PAIR, None),
        P(PAIR, SECTOR, None, None),
        P(PAIR, SECTOR, None, None),
        P(PAIR),
        P(SECTOR, None),
    )
    return jax.shard_map(
        per_device,
        mesh=split,
        in_specs=placed,
        out_specs=(P(SECTOR, PAIR, None), P(SECTOR, PAIR, None), P()),
        check_vma=False,
    )
```

profile of v0, /device:TPU:1, one launch (start us, length us, event | category | flops | bytes accessed | tf_op | source)
XLA Modules:
  0.0 650.0 jit_solution(17976514940221424542)
XLA Ops:
  7.2 4.5 collective-permute-start
  13.0 3.1 collective-permute-done.1
  28.1 128.5 %all-gather.3.cloned.1.call-done = f32[3,512,512]{2,1,0:T(8,128)} async-done(((f32[3,16,512]{2,1,0:T(8,128)}), f32[3,512,512]{2,1,0:T(8,128)}) %all-gather.3.cloned.1.call-update) | async-done | bytes 3145744 | tf_op jit(solution)/shard_map/all_gather | solution.py:23
  156.6 5.2 fusion.78
  162.2 3.5 fusion.21
  165.7 1.9 fusion.68
  167.7 2.2 fusion.23
  169.9 3.9 fusion.66
  173.8 3.5 fusion.18
  179.3 2.2 fusion.25
  181.5 3.7 fusion.54
  185.3 3.5 fusion.14
  189.0 23.1 %collective-permute-start.2 = (f32[512,512]{1,0:T(8,128)S(1)}, f32[512,512]{1,0:T(8,128)S(1)}, u32[]{:S(2)}, u32[]{:S(2)}) collective-permute-start(f32[512,512]{1,0:T(8,128)S(1)} %get-tuple-element.114), channel_id=1, source_target_pairs={{7,0},{0,1},{1,2},{2,3},{3,4},{4,5},{5,6},{6,7},{15,8},{8,9},{9,10... | collective-permute-start | bytes 3145736 | tf_op jit(solution)/shard_map/ppermute | solution.py:17
  214.0 12.9 %collective-permute-done.2 = f32[512,512]{1,0:T(8,128)S(1)} collective-permute-done((f32[512,512]{1,0:T(8,128)S(1)}, f32[512,512]{1,0:T(8,128)S(1)}, u32[]{:S(2)}, u32[]{:S(2)}) %collective-permute-start.2) | collective-permute-done | bytes 1048608 | tf_op jit(solution)/shard_map/ppermute | solution.py:17
  226.9 11.6 %collective-permute-done.3 = f32[512,512]{1,0:T(8,128)S(1)} collective-permute-done((f32[512,512]{1,0:T(8,128)S(1)}, f32[512,512]{1,0:T(8,128)S(1)}, u32[]{:S(2)}, u32[]{:S(2)}) %collective-permute-start.3) | collective-permute-done | bytes 1048608 | tf_op jit(solution)/shard_map/ppermute | solution.py:17
  238.5 2.0 fusion.37
  240.5 21.8 %all_to_all.10 = f32[32,1,16,512]{3,2,1,0:T(8,128)} all-to-all(f32[32,1,16,512]{3,2,1,0:T(8,128)S(1)} %bitcast.225), channel_id=1, replica_groups=mesh['pair_0'=2,'pair_1'=4,'pair_2'=4,'sector_0'=4,'sector_1'=2] {'pair_..., dimensions={0} | all-to-all | bytes 2097152 | tf_op jit(solution)/shard_map/all_to_all | solution.py:35
  264.2 4.5 all-reduce.14
  268.6 9.0 %all-reduce.8 = (f32[]{:T(128)}, f32[]{:T(128)}) all-reduce(f32[]{:T(128)} %get-tuple-element.109, f32[]{:T(128)} %get-tuple-element.110), channel_id=1, replica_groups=mesh['pair_0'=2,'pair_1'=4,'pair_2'=4,'sector_0'=4,'sector_1'=2] {'pair_1'}, use_global_device_ids=true, to_apply=%region_9.10 | all-reduce | flops 2 | bytes 16 | tf_op jit(solution)/shard_map/psum | solution.py:41
  277.7 7.0 %all-reduce.5 = (f32[]{:T(128)}, f32[]{:T(128)}) all-reduce(f32[]{:T(128)} %get-tuple-element.97, f32[]{:T(128)} %get-tuple-element.98), channel_id=1, replica_groups=mesh['pair_0'=2,'pair_1'=4,'pair_2'=4,'sector_0'=4,'sector_1'=2] {'pair_2'}, use_global_device_ids=true, to_apply=%region_10.11 | all-reduce | flops 2 | bytes 16 | tf_op jit(solution)/shard_map/psum | solution.py:41
  284.7 10.7 %all-reduce.2 = (f32[]{:T(128)}, f32[]{:T(128)}) all-reduce(f32[]{:T(128)} %get-tuple-element.91, f32[]{:T(128)} %get-tuple-element.92), channel_id=1, replica_groups=mesh['pair_0'=2,'pair_1'=4,'pair_2'=4,'sector_0'=4,'sector_1'=2] {'secto..., use_global_device_ids=true, to_apply=%region_11.12 | all-reduce | flops 2 | bytes 16 | tf_op jit(solution)/shard_map/psum | solution.py:41
  295.4 10.4 %all-reduce.11 = (f32[]{:T(128)}, f32[]{:T(128)}) all-reduce(f32[]{:T(128)} %get-tuple-element.85, f32[]{:T(128)} %get-tuple-element.86), channel_id=1, replica_groups=mesh['pair_0'=2,'pair_1'=4,'pair_2'=4,'sector_0'=4,'sector_1'=2] {'secto..., use_global_device_ids=true, to_apply=%region_12.13 | all-reduce | flops 2 | bytes 16 | tf_op jit(solution)/shard_map/psum | solution.py:41
  308.5 4.5 all-reduce.13
  313.0 7.8 %all-reduce.7 = (f32[]{:T(128)}, f32[]{:T(128)}) all-reduce(f32[]{:T(128)} %get-tuple-element.107, f32[]{:T(128)} %get-tuple-element.108), channel_id=1, replica_groups=mesh['pair_0'=2,'pair_1'=4,'pair_2'=4,'sector_0'=4,'sector_1'=2] {'pair_1'}, use_global_device_ids=true, to_apply=%region_21.22 | all-reduce | flops 2 | bytes 16 | tf_op jit(solution)/shard_map/psum | solution.py:41
  320.9 6.7 %all-reduce.4 = (f32[]{:T(128)}, f32[]{:T(128)}) all-reduce(f32[]{:T(128)} %get-tuple-element.95, f32[]{:T(128)} %get-tuple-element.96), channel_id=1, replica_groups=mesh['pair_0'=2,'pair_1'=4,'pair_2'=4,'sector_0'=4,'sector_1'=2] {'pair_2'}, use_global_device_ids=true, to_apply=%region_22.23 | all-reduce | flops 2 | bytes 16 | tf_op jit(solution)/shard_map/psum | solution.py:41
  327.5 9.3 %all-reduce.1 = (f32[]{:T(128)}, f32[]{:T(128)}) all-reduce(f32[]{:T(128)} %get-tuple-element.89, f32[]{:T(128)} %get-tuple-element.90), channel_id=1, replica_groups=mesh['pair_0'=2,'pair_1'=4,'pair_2'=4,'sector_0'=4,'sector_1'=2] {'secto..., use_global_device_ids=true, to_apply=%region_23.24 | all-reduce | flops 2 | bytes 16 | tf_op jit(solution)/shard_map/psum | solution.py:41
  336.9 10.1 %all-reduce.10 = (f32[]{:T(128)}, f32[]{:T(128)}) all-reduce(f32[]{:T(128)} %get-tuple-element.83, f32[]{:T(128)} %get-tuple-element.84), channel_id=1, replica_groups=mesh['pair_0'=2,'pair_1'=4,'pair_2'=4,'sector_0'=4,'sector_1'=2] {'secto..., use_global_device_ids=true, to_apply=%region_24.25 | all-reduce | flops 2 | bytes 16 | tf_op jit(solution)/shard_map/psum | solution.py:41
  351.8 3.5 collective-permute-done.5
  356.0 134.3 %all-gather.5.cloned.1.call-done = f32[3,512,512]{2,1,0:T(8,128)} async-done(((f32[3,16,512]{2,1,0:T(8,128)}), f32[3,512,512]{2,1,0:T(8,128)}) %all-gather.5.cloned.1.call-update) | async-done | bytes 3145744 | tf_op jit(solution)/shard_map/all_gather | solution.py:23
  490.2 4.8 fusion.75
  495.5 3.5 fusion.10
  499.0 1.9 fusion.42
  501.0 2.2 fusion.29
  503.2 3.7 fusion.63
  506.9 3.5 fusion.7
  512.4 2.2 fusion.31
  514.6 3.8 fusion.51
  518.4 3.5 fusion.3
  522.1 23.0 %collective-permute-start.6 = (f32[512,512]{1,0:T(8,128)S(1)}, f32[512,512]{1,0:T(8,128)S(1)}, u32[]{:S(2)}, u32[]{:S(2)}) collective-permute-start(f32[512,512]{1,0:T(8,128)S(1)} %get-tuple-element.112), channel_id=1, source_target_pairs={{7,0},{0,1},{1,2},{2,3},{3,4},{4,5},{5,6},{6,7},{15,8},{8,9},{9,10... | collective-permute-start | bytes 3145736 | tf_op jit(solution)/shard_map/ppermute | solution.py:17
  547.0 12.9 %collective-permute-done.6 = f32[512,512]{1,0:T(8,128)S(1)} collective-permute-done((f32[512,512]{1,0:T(8,128)S(1)}, f32[512,512]{1,0:T(8,128)S(1)}, u32[]{:S(2)}, u32[]{:S(2)}) %collective-permute-start.6) | collective-permute-done | bytes 1048608 | tf_op jit(solution)/shard_map/ppermute | solution.py:17
  559.9 11.6 %collective-permute-done.7 = f32[512,512]{1,0:T(8,128)S(1)} collective-permute-done((f32[512,512]{1,0:T(8,128)S(1)}, f32[512,512]{1,0:T(8,128)S(1)}, u32[]{:S(2)}, u32[]{:S(2)}) %collective-permute-start.7) | collective-permute-done | bytes 1048608 | tf_op jit(solution)/shard_map/ppermute | solution.py:17
  571.5 2.0 fusion.35
  573.5 21.8 %all_to_all.11 = f32[32,1,16,512]{3,2,1,0:T(8,128)S(1)} all-to-all(f32[32,1,16,512]{3,2,1,0:T(8,128)S(1)} %bitcast.224), channel_id=1, replica_groups=mesh['pair_0'=2,'pair_1'=4,'pair_2'=4,'sector_0'=4,'sector_1'=2] {'pair_..., dimensions={0} | all-to-all | bytes 2097152 | tf_op jit(solution)/shard_map/all_to_all | solution.py:35
  596.0 4.4 all-reduce.12
  600.4 9.0 %all-reduce.6 = (f32[]{:T(128)}, f32[]{:T(128)}) all-reduce(f32[]{:T(128)} %get-tuple-element.105, f32[]{:T(128)} %get-tuple-element.106), channel_id=1, replica_groups=mesh['pair_0'=2,'pair_1'=4,'pair_2'=4,'sector_0'=4,'sector_1'=2] {'pair_1'}, use_global_device_ids=true, to_apply=%region_34.35 | all-reduce | flops 2 | bytes 16 | tf_op jit(solution)/shard_map/psum | solution.py:41
  609.4 6.9 %all-reduce.3 = (f32[]{:T(128)}, f32[]{:T(128)}) all-reduce(f32[]{:T(128)} %get-tuple-element.93, f32[]{:T(128)} %get-tuple-element.94), channel_id=1, replica_groups=mesh['pair_0'=2,'pair_1'=4,'pair_2'=4,'sector_0'=4,'sector_1'=2] {'pair_2'}, use_global_device_ids=true, to_apply=%region_35.36 | all-reduce | flops 2 | bytes 16 | tf_op jit(solution)/shard_map/psum | solution.py:41
  616.4 10.8 %all-reduce = (f32[]{:T(128)}, f32[]{:T(128)}) all-reduce(f32[]{:T(128)} %get-tuple-element.87, f32[]{:T(128)} %get-tuple-element.88), channel_id=1, replica_groups=mesh['pair_0'=2,'pair_1'=4,'pair_2'=4,'sector_0'=4,'sector_1'=2] {'secto..., use_global_device_ids=true, to_apply=%region_36.37 | all-reduce | flops 2 | bytes 16 | tf_op jit(solution)/shard_map/psum | solution.py:41
  627.1 10.4 %all-reduce.9 = (f32[]{:T(128)}, f32[]{:T(128)}) all-reduce(f32[]{:T(128)} %get-tuple-element.81, f32[]{:T(128)} %get-tuple-element.82), channel_id=1, replica_groups=mesh['pair_0'=2,'pair_1'=4,'pair_2'=4,'sector_0'=4,'sector_1'=2] {'secto..., use_global_device_ids=true, to_apply=%region_37.38 | all-reduce | flops 2 | bytes 16 | tf_op jit(solution)/shard_map/psum | solution.py:41
  (49 shorter events, 22.6 us)
Async XLA Ops:
  7.2 149.5 %all-gather.3.cloned.1.call-start = ((), (), s32[]{:S(2)}) async-start(), calls=%async_computation.2 | async-start | bytes 3244032 | tf_op jit(solution)/shard_map/all_gather | solution.py:23
  7.2 5.8 collective-permute-start
  11.7 4.4 collective-permute-start.1
  17.5 472.7 %all-gather.5.cloned.1.call-start = ((), (), s32[]{:S(2)}) async-start(), calls=%async_computation.3 | async-start | bytes 3244032 | tf_op jit(solution)/shard_map/all_gather | solution.py:23
  156.6 5.6 copy-start.1
  161.8 3.9 copy-start
  161.8 3.9 copy-start.3
  189.0 37.9 %collective-permute-start.2 = (f32[512,512]{1,0:T(8,128)S(1)}, f32[512,512]{1,0:T(8,128)S(1)}, u32[]{:S(2)}, u32[]{:S(2)}) collective-permute-start(f32[512,512]{1,0:T(8,128)S(1)} %get-tuple-element.114), channel_id=1, source_target_pairs={{7,0},{0,1},{1,2},{2,3},{3,4},{4,5},{5,6},{6,7},{15,8},{8,9},{9,10... | collective-permute-start | bytes 3145736 | tf_op jit(solution)/shard_map/ppermute | solution.py:17
  212.0 26.4 %collective-permute-start.3 = (f32[512,512]{1,0:T(8,128)S(1)}, f32[512,512]{1,0:T(8,128)S(1)}, u32[]{:S(2)}, u32[]{:S(2)}) collective-permute-start(f32[512,512]{1,0:T(8,128)S(1)} %get-tuple-element.115), channel_id=1, source_target_pairs={{1,0},{2,1},{3,2},{4,3},{5,4},{6,5},{7,6},{0,7},{9,8},{10,9},{11,1... | collective-permute-start | bytes 3145736 | tf_op jit(solution)/shard_map/ppermute | solution.py:17
  240.4 23.1 %copy-start.5 = (f32[1,16,512]{2,1,0:T(8,128)S(1)}, f32[1,16,512]{2,1,0:T(8,128)}, u32[]{:S(2)}) copy-start(f32[1,16,512]{2,1,0:T(8,128)} %param.18) | copy-start | bytes 98308
  240.4 67.5 %copy-start.6 = (f32[1,16,512]{2,1,0:T(8,128)S(1)}, f32[1,16,512]{2,1,0:T(8,128)}, u32[]{:S(2)}) copy-start(f32[1,16,512]{2,1,0:T(8,128)} %param.19) | copy-start | bytes 98308
  349.6 2.2 collective-permute-start.4
  350.8 4.5 collective-permute-start.5
  490.2 5.3 copy-start.2
  495.1 3.9 copy-start.4
  522.1 37.8 %collective-permute-start.6 = (f32[512,512]{1,0:T(8,128)S(1)}, f32[512,512]{1,0:T(8,128)S(1)}, u32[]{:S(2)}, u32[]{:S(2)}) collective-permute-start(f32[512,512]{1,0:T(8,128)S(1)} %get-tuple-element.112), channel_id=1, source_target_pairs={{7,0},{0,1},{1,2},{2,3},{3,4},{4,5},{5,6},{6,7},{15,8},{8,9},{9,10... | collective-permute-start | bytes 3145736 | tf_op jit(solution)/shard_map/ppermute | solution.py:17
  545.1 26.4 %collective-permute-start.7 = (f32[512,512]{1,0:T(8,128)S(1)}, f32[512,512]{1,0:T(8,128)S(1)}, u32[]{:S(2)}, u32[]{:S(2)}) collective-permute-start(f32[512,512]{1,0:T(8,128)S(1)} %get-tuple-element.113), channel_id=1, source_target_pairs={{1,0},{2,1},{3,2},{4,3},{5,4},{6,5},{7,6},{0,7},{9,8},{10,9},{11,1... | collective-permute-start | bytes 3145736 | tf_op jit(solution)/shard_map/ppermute | solution.py:17
Sparse Core Ops, SparseCore 0:
  17.7 138.9 all-gather.2
  356.1 134.1 all-gather.4
where the time goes:
time: 660 us; the launch traced here: 650 us
  waiting for transfers between devices  321 us (49%)
  blocking collectives  165 us (25%)
  matrix products  70.3 us (11%)
  starting transfers between devices  51.8 us (8%)
  between operations  30.7 us (5%)
  other arithmetic  7.11 us (1%)
    all_gather x2, waiting for transfers between devices, side_by_side(): out = lax.all_gather(both, axis, axis=dim, tiled=True)  263 us
    psum x15, blocking collectives, by_axis(): value = lax.psum(value, axis)  122 us
    dot_general x24, matrix products, product(): jnp.dot(first, second, precision=highest, preferred_element_type=jnp.floa...  70.3 us
    ppermute x8, waiting for transfers between devices, shifted(): return lax.ppermute(block, axis, route)  57.9 us
    ppermute x8, starting transfers between devices, shifted(): return lax.ppermute(block, axis, route)  51.7 us
    all_to_all x2, blocking collectives, sum_at_owner(): lax.all_to_all(cut_along(value, dim, peers), axis, 0, 0, tiled=True)  43.6 us
  transfers between devices with their start and end apart: 10, of which 10 were waited for; matrix products, arithmetic and copies ran while one was open for 1% of the time, Pallas kernels for 0%

commit v1 on v0

--- a/solution.py
+++ b/solution.py
@@ -38,7 +38,7 @@
 
 def by_axis(value, axes):
     for axis in axes:
-        value = lax.psum(value, axis)
+        value = jnp.sum(lax.all_gather(value, axis), axis=0)
     return value
 
 

time: 660 us -> 726 us (1.10)
  local copies, waits for them, and re-layouts: 4.18 us -> 47.7 us
  blocking collectives: 165 us -> 134 us
  other arithmetic: 7.11 us -> 25.8 us
  waiting for transfers between devices: 321 us -> 336 us
  matrix products: 70.3 us -> 83 us
    psum x15 -> x0, blocking collectives: 122 us -> none  [by_axis(): value = lax.psum(value, axis)]
    unnamed x0 -> x15, blocking collectives: none -> 112 us
    unnamed x14 -> x89, local copies, waits for them, and re-layouts: 0.03 us -> 43.6 us
    all_to_all x2 -> x1, blocking collectives: 43.6 us -> 21.8 us  [sum_at_owner(): lax.all_to_all(cut_along(value, dim, peers), axis, 0, 0, tiled=True)]
    reduce_sum x0 -> x30, other arithmetic: none -> 18.5 us  [by_axis(): value = jnp.sum(lax.all_gather(value, axis), axis=0)]
    all_to_all x0 -> x1, waiting for transfers between devices: none -> 15.2 us  [sum_at_owner(): lax.all_to_all(cut_along(value, dim, peers), axis, 0, 0, tiled=True)]
    dot_general x24, matrix products: 70.3 us -> 83 us  [product(): jnp.dot(first, second, precision=highest, preferred_element_type=jnp.floa...]
  transfers between devices with their start and end apart: 10 -> 11, of which waited for: 10 -> 11; matrix products, arithmetic and copies ran while one was open for 1% -> 1% of each run, Pallas kernels for 0% -> 0%
where the time goes in v1:
time: 726 us; the launch traced here: 715 us
  waiting for transfers between devices  336 us (46%)
  blocking collectives  134 us (18%)
  matrix products  83 us (11%)
  starting transfers between devices  58.1 us (8%)
  local copies, waits for them, and re-layouts  47.7 us (7%)
  between operations  30.8 us (4%)
  other arithmetic  25.8 us (4%)
    all_gather x2, waiting for transfers between devices, side_by_side(): out = lax.all_gather(both, axis, axis=dim, tiled=True)  263 us
    unnamed x15, blocking collectives  112 us
    dot_general x24, matrix products, product(): jnp.dot(first, second, precision=highest, preferred_element_type=jnp.floa...  83 us
    ppermute x8, waiting for transfers between devices, shifted(): return lax.ppermute(block, axis, route)  57.7 us
    ppermute x8, starting transfers between devices, shifted(): return lax.ppermute(block, axis, route)  51.7 us
    unnamed x89, local copies, waits for them, and re-layouts  43.6 us
    all_to_all x1, blocking collectives, sum_at_owner(): lax.all_to_all(cut_along(value, dim, peers), axis, 0, 0, tiled=True)  21.8 us
    reduce_sum x30, other arithmetic, by_axis(): value = jnp.sum(lax.all_gather(value, axis), axis=0)  18.5 us
  transfers between devices with their start and end apart: 11, of which 11 were waited for; matrix products, arithmetic and copies ran while one was open for 1% of the time, Pallas kernels for 0%

profile of v1, /device:TPU:1, one launch (start us, length us, event | category | flops | bytes accessed | tf_op | source)
XLA Modules:
  0.0 715.2 jit_solution(2061353207486023864)
XLA Ops:
  7.2 4.5 collective-permute-start
  13.0 3.1 collective-permute-done.1
  28.0 128.6 %all-gather.3.cloned.1.call-done = f32[3,512,512]{2,1,0:T(8,128)} async-done(((f32[3,16,512]{2,1,0:T(8,128)}), f32[3,512,512]{2,1,0:T(8,128)}) %all-gather.3.cloned.1.call-update) | async-done | bytes 3145744 | tf_op jit(solution)/shard_map/all_gather | solution.py:23
  156.6 5.2 fusion.78
  162.2 3.5 fusion.21
  167.7 2.2 fusion.23
  169.9 3.8 fusion.66
  173.8 3.5 fusion.18
  179.2 2.2 fusion.25
  181.4 15.5 %fusion.54 = f32[512,512]{1,0:T(8,128)S(1)} fusion(f32[3,512,512]{2,1,0:T(8,128)S(1)} %copy-done.3, f32[3,1,512,512]{3,2,1,0:T(8,128)S(1)} %copy-done), kind=kOutput, calls=%fused_computation.72 | convolution fusion | flops 1610612736 | bytes 3145728 | tf_op jit(solution)/shard_map/dot_general | solution.py:46
  196.9 3.5 fusion.14
  200.6 23.0 %collective-permute-start.2 = (f32[512,512]{1,0:T(8,128)S(1)}, f32[512,512]{1,0:T(8,128)S(1)}, u32[]{:S(2)}, u32[]{:S(2)}) collective-permute-start(f32[512,512]{1,0:T(8,128)S(1)} %get-tuple-element.114), channel_id=1, source_target_pairs={{7,0},{0,1},{1,2},{2,3},{3,4},{4,5},{5,6},{6,7},{15,8},{8,9},{9,10... | collective-permute-start | bytes 3145736 | tf_op jit(solution)/shard_map/ppermute | solution.py:17
  225.6 12.9 %collective-permute-done.2 = f32[512,512]{1,0:T(8,128)S(1)} collective-permute-done((f32[512,512]{1,0:T(8,128)S(1)}, f32[512,512]{1,0:T(8,128)S(1)}, u32[]{:S(2)}, u32[]{:S(2)}) %collective-permute-start.2) | collective-permute-done | bytes 1048608 | tf_op jit(solution)/shard_map/ppermute | solution.py:17
  238.4 11.7 %collective-permute-done.3 = f32[512,512]{1,0:T(8,128)S(1)} collective-permute-done((f32[512,512]{1,0:T(8,128)S(1)}, f32[512,512]{1,0:T(8,128)S(1)}, u32[]{:S(2)}, u32[]{:S(2)}) %collective-permute-start.3) | collective-permute-done | bytes 1048608 | tf_op jit(solution)/shard_map/ppermute | solution.py:17
  250.1 3.1 fusion.37
  253.2 6.4 all-to-all-start
  260.2 15.2 %all-to-all-done = f32[32,1,16,512]{3,2,1,0:T(8,128)} async-done(((f32[32,1,16,512]{3,2,1,0:T(8,128)}), f32[32,1,16,512]{3,2,1,0:T(8,128)}, u32[]{:S(2)}, u32[]{:S(2)}) %all-to-all-start) | async-done | bytes 1048608 | tf_op jit(solution)/shard_map/all_to_all | solution.py:35
  280.7 3.8 all-reduce.44
  289.0 8.4 %all-reduce.38 = (f32[4]{0:T(128)S(1)}, f32[4]{0:T(128)S(1)}) all-reduce(f32[4]{0:T(128)S(1)} %dynamic-update-slice.24, f32[4]{0:T(128)S(1)} %dynamic-update-slice.19), channel_id=1, replica_groups=mesh['pair_0'=2,'pair_1'=4,'pair_2'=4,'sector_0'=4,'sector_1'=2] {'pair_1'}, use_global_device_ids=true, to_apply=%add.6 | all-reduce | flops 8 | bytes 64
  302.1 6.3 all-reduce.35
  313.1 10.1 %all-reduce.32 = (f32[4]{0:T(128)S(1)}, f32[4]{0:T(128)S(1)}) all-reduce(f32[4]{0:T(128)S(1)} %dynamic-update-slice.26, f32[4]{0:T(128)S(1)} %dynamic-update-slice.21), channel_id=1, replica_groups=mesh['pair_0'=2,'pair_1'=4,'pair_2'=4,'sector_0'=4,'sector_1'=2] {'secto..., use_global_device_ids=true, to_apply=%add.8 | all-reduce | flops 8 | bytes 64
  327.1 9.7 %all-reduce.41 = (f32[2]{0:T(128)S(1)}, f32[2]{0:T(128)S(1)}) all-reduce(f32[2]{0:T(128)S(1)} %dynamic-update-slice.27, f32[2]{0:T(128)S(1)} %dynamic-update-slice.22), channel_id=1, replica_groups=mesh['pair_0'=2,'pair_1'=4,'pair_2'=4,'sector_0'=4,'sector_1'=2] {'secto..., use_global_device_ids=true, to_apply=%add.9 | all-reduce | flops 4 | bytes 32
  343.5 3.8 all-reduce.43
  351.1 7.2 %all-reduce.37 = (f32[4]{0:T(128)S(1)}, f32[4]{0:T(128)S(1)}) all-reduce(f32[4]{0:T(128)S(1)} %dynamic-update-slice.34, f32[4]{0:T(128)S(1)} %dynamic-update-slice.29), channel_id=1, replica_groups=mesh['pair_0'=2,'pair_1'=4,'pair_2'=4,'sector_0'=4,'sector_1'=2] {'pair_1'}, use_global_device_ids=true, to_apply=%add.16 | all-reduce | flops 8 | bytes 64
  362.3 6.0 all-reduce.34
  372.3 8.6 %all-reduce.31 = (f32[4]{0:T(128)S(1)}, f32[4]{0:T(128)S(1)}) all-reduce(f32[4]{0:T(128)S(1)} %dynamic-update-slice.36, f32[4]{0:T(128)S(1)} %dynamic-update-slice.31), channel_id=1, replica_groups=mesh['pair_0'=2,'pair_1'=4,'pair_2'=4,'sector_0'=4,'sector_1'=2] {'secto..., use_global_device_ids=true, to_apply=%add.18 | all-reduce | flops 8 | bytes 64
  384.7 9.4 %all-reduce.40 = (f32[2]{0:T(128)S(1)}, f32[2]{0:T(128)S(1)}) all-reduce(f32[2]{0:T(128)S(1)} %dynamic-update-slice.37, f32[2]{0:T(128)S(1)} %dynamic-update-slice.32), channel_id=1, replica_groups=mesh['pair_0'=2,'pair_1'=4,'pair_2'=4,'sector_0'=4,'sector_1'=2] {'secto..., use_global_device_ids=true, to_apply=%add.19 | all-reduce | flops 4 | bytes 32
  400.0 3.7 collective-permute-done.5
  404.3 134.5 %all-gather.5.cloned.1.call-done = f32[3,512,512]{2,1,0:T(8,128)} async-done(((f32[3,16,512]{2,1,0:T(8,128)}), f32[3,512,512]{2,1,0:T(8,128)}) %all-gather.5.cloned.1.call-update) | async-done | bytes 3145744 | tf_op jit(solution)/shard_map/all_gather | solution.py:23
  538.8 4.8 fusion.75
  544.1 3.5 fusion.10
  549.5 2.2 fusion.29
  551.7 3.7 fusion.63
  555.5 3.5 fusion.7
  559.0 1.9 fusion.40
  560.9 2.2 fusion.31
  563.2 3.8 fusion.51
  567.0 3.5 fusion.3
  570.6 23.0 %collective-permute-start.6 = (f32[512,512]{1,0:T(8,128)S(1)}, f32[512,512]{1,0:T(8,128)S(1)}, u32[]{:S(2)}, u32[]{:S(2)}) collective-permute-start(f32[512,512]{1,0:T(8,128)S(1)} %get-tuple-element.112), channel_id=1, source_target_pairs={{7,0},{0,1},{1,2},{2,3},{3,4},{4,5},{5,6},{6,7},{15,8},{8,9},{9,10... | collective-permute-start | bytes 3145736 | tf_op jit(solution)/shard_map/ppermute | solution.py:17
  595.6 12.9 %collective-permute-done.6 = f32[512,512]{1,0:T(8,128)S(1)} collective-permute-done((f32[512,512]{1,0:T(8,128)S(1)}, f32[512,512]{1,0:T(8,128)S(1)}, u32[]{:S(2)}, u32[]{:S(2)}) %collective-permute-start.6) | collective-permute-done | bytes 1048608 | tf_op jit(solution)/shard_map/ppermute | solution.py:17
  608.4 11.6 %collective-permute-done.7 = f32[512,512]{1,0:T(8,128)S(1)} collective-permute-done((f32[512,512]{1,0:T(8,128)S(1)}, f32[512,512]{1,0:T(8,128)S(1)}, u32[]{:S(2)}, u32[]{:S(2)}) %collective-permute-start.7) | collective-permute-done | bytes 1048608 | tf_op jit(solution)/shard_map/ppermute | solution.py:17
  620.0 2.0 fusion.35
  622.1 21.8 %all_to_all.10 = f32[32,1,16,512]{3,2,1,0:T(8,128)S(1)} all-to-all(f32[32,1,16,512]{3,2,1,0:T(8,128)S(1)} %bitcast.260), channel_id=1, replica_groups=mesh['pair_0'=2,'pair_1'=4,'pair_2'=4,'sector_0'=4,'sector_1'=2] {'pair_..., dimensions={0} | all-to-all | bytes 2097152 | tf_op jit(solution)/shard_map/all_to_all | solution.py:35
  647.2 3.8 all-reduce.42
  654.8 8.4 %all-reduce.36 = (f32[4]{0:T(128)S(1)}, f32[4]{0:T(128)S(1)}) all-reduce(f32[4]{0:T(128)S(1)} %dynamic-update-slice.44, f32[4]{0:T(128)S(1)} %dynamic-update-slice.39), channel_id=1, replica_groups=mesh['pair_0'=2,'pair_1'=4,'pair_2'=4,'sector_0'=4,'sector_1'=2] {'pair_1'}, use_global_device_ids=true, to_apply=%add.26 | all-reduce | flops 8 | bytes 64
  667.2 6.3 all-reduce.33
  677.4 10.0 %all-reduce.30 = (f32[4]{0:T(128)S(1)}, f32[4]{0:T(128)S(1)}) all-reduce(f32[4]{0:T(128)S(1)} %dynamic-update-slice.46, f32[4]{0:T(128)S(1)} %dynamic-update-slice.41), channel_id=1, replica_groups=mesh['pair_0'=2,'pair_1'=4,'pair_2'=4,'sector_0'=4,'sector_1'=2] {'secto..., use_global_device_ids=true, to_apply=%add.28 | all-reduce | flops 8 | bytes 64
  691.3 10.2 %all-reduce.39 = (f32[2]{0:T(128)S(1)}, f32[2]{0:T(128)S(1)}) all-reduce(f32[2]{0:T(128)S(1)} %dynamic-update-slice.47, f32[2]{0:T(128)S(1)} %dynamic-update-slice.42), channel_id=1, replica_groups=mesh['pair_0'=2,'pair_1'=4,'pair_2'=4,'sector_0'=4,'sector_1'=2] {'secto..., use_global_device_ids=true, to_apply=%add.29 | all-reduce | flops 4 | bytes 32
  (155 shorter events, 86.4 us)
Async XLA Ops:
  7.2 149.5 %all-gather.3.cloned.1.call-start = ((), (), s32[]{:S(2)}) async-start(), calls=%async_computation.2 | async-start | bytes 3244032 | tf_op jit(solution)/shard_map/all_gather | solution.py:23
  7.2 5.8 collective-permute-start
  11.7 4.4 collective-permute-start.1
  156.6 5.6 copy-start.1
  161.8 3.9 copy-start
  161.8 3.9 copy-start.3
  200.6 37.8 %collective-permute-start.2 = (f32[512,512]{1,0:T(8,128)S(1)}, f32[512,512]{1,0:T(8,128)S(1)}, u32[]{:S(2)}, u32[]{:S(2)}) collective-permute-start(f32[512,512]{1,0:T(8,128)S(1)} %get-tuple-element.114), channel_id=1, source_target_pairs={{7,0},{0,1},{1,2},{2,3},{3,4},{4,5},{5,6},{6,7},{15,8},{8,9},{9,10... | collective-permute-start | bytes 3145736 | tf_op jit(solution)/shard_map/ppermute | solution.py:17
  223.6 26.5 %collective-permute-start.3 = (f32[512,512]{1,0:T(8,128)S(1)}, f32[512,512]{1,0:T(8,128)S(1)}, u32[]{:S(2)}, u32[]{:S(2)}) collective-permute-start(f32[512,512]{1,0:T(8,128)S(1)} %get-tuple-element.115), channel_id=1, source_target_pairs={{1,0},{2,1},{3,2},{4,3},{5,4},{6,5},{7,6},{0,7},{9,8},{10,9},{11,1... | collective-permute-start | bytes 3145736 | tf_op jit(solution)/shard_map/ppermute | solution.py:17
  225.6 34.1 %copy-start.11 = (u32[256]{0:T(256)S(1)}, u32[256]{0:T(256)}, u32[]{:S(2)}) copy-start(u32[256]{0:T(256)} %constant.208) | copy-start | bytes 3076
  253.2 23.5 %copy-start.5 = (f32[1,16,512]{2,1,0:T(8,128)S(1)}, f32[1,16,512]{2,1,0:T(8,128)}, u32[]{:S(2)}) copy-start(f32[1,16,512]{2,1,0:T(8,128)} %param.18) | copy-start | bytes 98308
  253.2 26.9 %copy-start.10 = (u32[256]{0:T(256)S(1)}, u32[256]{0:T(256)}, u32[]{:S(2)}) copy-start(u32[256]{0:T(256)} %constant.213) | copy-start | bytes 3076
  253.2 35.2 %copy-start.9 = (u32[256]{0:T(256)S(1)}, u32[256]{0:T(256)}, u32[]{:S(2)}) copy-start(u32[256]{0:T(256)} %constant.218) | copy-start | bytes 3076
  253.2 48.3 %copy-start.8 = (u32[256]{0:T(256)S(1)}, u32[256]{0:T(256)}, u32[]{:S(2)}) copy-start(u32[256]{0:T(256)} %constant.223) | copy-start | bytes 3076
  253.2 59.3 %copy-start.7 = (u32[256]{0:T(256)S(1)}, u32[256]{0:T(256)}, u32[]{:S(2)}) copy-start(u32[256]{0:T(256)} %constant.228) | copy-start | bytes 3076
  253.2 86.9 %copy-start.6 = (f32[1,16,512]{2,1,0:T(8,128)S(1)}, f32[1,16,512]{2,1,0:T(8,128)}, u32[]{:S(2)}) copy-start(f32[1,16,512]{2,1,0:T(8,128)} %param.19) | copy-start | bytes 98308
  253.2 22.2 %all-to-all-start = ((f32[32,1,16,512]{3,2,1,0:T(8,128)}), f32[32,1,16,512]{3,2,1,0:T(8,128)}, u32[]{:S(2)}, u32[]{:S(2)}) async-start(f32[32,1,16,512]{3,2,1,0:T(8,128)} %bitcast.259), calls=%async_computation | async-start | bytes 2097152 | tf_op jit(solution)/shard_map/all_to_all | solution.py:35
  259.6 279.2 %all-gather.5.cloned.1.call-start = ((), (), s32[]{:S(2)}) async-start(), calls=%async_computation.3 | async-start | bytes 3244032 | tf_op jit(solution)/shard_map/all_gather | solution.py:23
  398.2 1.8 collective-permute-start.4
  399.0 4.7 collective-permute-start.5
  538.8 5.3 copy-start.2
  543.6 3.9 copy-start.4
  570.6 37.8 %collective-permute-start.6 = (f32[512,512]{1,0:T(8,128)S(1)}, f32[512,512]{1,0:T(8,128)S(1)}, u32[]{:S(2)}, u32[]{:S(2)}) collective-permute-start(f32[512,512]{1,0:T(8,128)S(1)} %get-tuple-element.112), channel_id=1, source_target_pairs={{7,0},{0,1},{1,2},{2,3},{3,4},{4,5},{5,6},{6,7},{15,8},{8,9},{9,10... | collective-permute-start | bytes 3145736 | tf_op jit(solution)/shard_map/ppermute | solution.py:17
  593.7 26.4 %collective-permute-start.7 = (f32[512,512]{1,0:T(8,128)S(1)}, f32[512,512]{1,0:T(8,128)S(1)}, u32[]{:S(2)}, u32[]{:S(2)}) collective-permute-start(f32[512,512]{1,0:T(8,128)S(1)} %get-tuple-element.113), channel_id=1, source_target_pairs={{1,0},{2,1},{3,2},{4,3},{5,4},{6,5},{7,6},{0,7},{9,8},{10,9},{11,1... | collective-permute-start | bytes 3145736 | tf_op jit(solution)/shard_map/ppermute | solution.py:17
Sparse Core Ops, SparseCore 0:
  17.7 138.9 all-gather.2
  404.4 134.2 all-gather.4
